TPU v7x, 128 devices: a whole 4x4x4 slice. The times are simulated.
128 devices in a mesh: grp: 2 (over x_hi), gx: 16 (over z, y), gy: 4 (over x_lo, core).
Axes of the slice: x: 4 (x_hi: 2, x_lo: 2; x = x_hi * 2 + x_lo), y: 4, z: 4, core: 2. Of those that a mesh axis runs over, the one named last changes fastest.
Arguments:
- tracers: float32 [256, 1024, 1536], P('grp', 'gx', 'gy'), may hold values from -6 to 6
- dycore_air_mass: float32 [512, 16, 384], P(('grp', 'gx', 'gy')), may hold values from 1 to 2
- dycore_face_flux: float32 [512, 2, 16, 384], P(('grp', 'gx', 'gy')), may hold values from -0.2 to 0.2
- tile_dycore_slot: int32 [256], replicated, may hold values from 0 to 511, as said below
- water_idx: int32 [6], replicated, may hold values from 0 to 255, as said below
Outputs:
- new_tracers: float32 [256, 1024, 1536], P('grp', 'gx', 'gy')
- water_to_dycore: float32 [512, 6, 16, 384], P(('grp', 'gx', 'gy'))
Inputs may be any that keep to these rules, and one draw needn't show every extreme that they name: `tile_dycore_slot`: slot g lies on dycore device g // 4, devices in the order grp, gx, gy. Entries are distinct; a device's tiles fill its first slots in the order of the tiles. The tiles of block b lie on distinct dycore devices whose gx index is b // 4; in every gx index some device holds 4 tiles. `water_idx`: distinct tracer numbers; 0 and 255 are always among them.
All inputs are finite; a program needn't handle non-finite values.
Results may differ from a plain program's by a relative error of at most 0.0003.
Values sent between devices are 32-bit elements; how exact they have to be, the bound alone decides.
A program may use at most 256 MiB of HBM per device.

v0:
```python
import jax
import jax.numpy as jnp
from jax import lax
from jax.sharding import PartitionSpec as P

TPB = 4
PEER = 1
NSUB = 2


def extended(block, sides, width):
    for axis, dim in sides:
        count = lax.axis_size(axis)
        forward = [(i, i + 1) for i in range(count - 1)]
        backward = [(target, source) for source, target in forward]
        low = lax.ppermute(
            lax.slice_in_dim(block, block.shape[dim] - width, None, axis=dim), axis, forward
        )
        high = lax.ppermute(lax.slice_in_dim(block, 0, width, axis=dim), axis, backward)
        block = jnp.concatenate([low, block, high], axis=dim)
    return block


def upwind_faces(behind_one, centre, ahead_one, ahead_two, flow):
    from_left = (-behind_one + 5.0 * centre + 2.0 * ahead_one) / 6.0
    from_right = (2.0 * centre + 5.0 * ahead_one - ahead_two) / 6.0
    return flow * jnp.where(flow > 0, from_left, from_right)


def mass_update(flow_x_pad, flow_y_pad, air_mass):
    cells_x, cells_y = air_mass.shape
    east = flow_x_pad[1 : cells_x + 2, 2 : cells_y + 2]
    north = flow_y_pad[2 : cells_x + 2, 1 : cells_y + 2]
    return air_mass - (east[1:] - east[:-1]) - (north[:, 1:] - north[:, :-1])


def advance(padded, flow_x_pad, flow_y_pad, air_mass, mass_next):
    cells_x, cells_y = air_mass.shape
    along_x = padded[:, :, 2 : cells_y + 2]
    east = flow_x_pad[1 : cells_x + 2, 2 : cells_y + 2]
    flux_x = upwind_faces(
        along_x[:, 0 : cells_x + 1],
        along_x[:, 1 : cells_x + 2],
        along_x[:, 2 : cells_x + 3],
        along_x[:, 3 : cells_x + 4],
        east,
    )
    along_y = padded[:, 2 : cells_x + 2, :]
    north = flow_y_pad[2 : cells_x + 2, 1 : cells_y + 2]
    flux_y = upwind_faces(
        along_y[:, :, 0 : cells_y + 1],
        along_y[:, :, 1 : cells_y + 2],
        along_y[:, :, 2 : cells_y + 3],
        along_y[:, :, 3 : cells_y + 4],
        north,
    )
    centre = padded[:, 2 : cells_x + 2, 2 : cells_y + 2]
    return (
        air_mass * centre
        - (flux_x[:, 1:] - flux_x[:, :-1])
        - (flux_y[:, :, 1:] - flux_y[:, :, :-1])
    ) / mass_next


def route_rows(targets, count):
    return (targets[None, :] == jnp.arange(count, dtype=jnp.int32)[:, None]).astype(jnp.float32)


def pair_ranks(owners, tile_count):
    grouped = owners.reshape(-1, tile_count)
    same = grouped[:, :, None] == grouped[:, None, :]
    earlier = jnp.arange(tile_count)[None, :] < jnp.arange(tile_count)[:, None]
    return jnp.sum(same & earlier[None], axis=2).reshape(-1)


def per_device(tracers, dycore_air_mass, dycore_face_flux, tile_dycore_slot, water_idx):
    block_count = lax.axis_size(("gx", "gy"))
    column_count = lax.axis_size("gy")
    group_count = lax.axis_size(("grp", "gy"))
    my_device = lax.axis_index(("grp", "gx", "gy"))
    my_block = lax.axis_index(("gx", "gy"))
    my_half = lax.axis_index("grp")
    slot_count = dycore_air_mass.shape[0]
    band_rows = dycore_air_mass.shape[1]
    cells_y = dycore_air_mass.shape[2]
    tile_total = tile_dycore_slot.shape[0]
    highest = lax.Precision.HIGHEST
    owners = tile_dycore_slot // slot_count
    slot_index = tile_dycore_slot % slot_count
    owner_local = owners // block_count * column_count + owners % column_count
    tile_ids = jnp.arange(tile_total, dtype=jnp.int32)
    block_col = tile_ids // TPB % column_count
    pair_rank = pair_ranks(owners, TPB)
    is_mine = owners == my_device
    slot_hot = (
        (slot_index[:, None] == jnp.arange(slot_count, dtype=jnp.int32)[None, :]) & is_mine[:, None]
    ).astype(jnp.float32)
    own_local = lax.dynamic_slice_in_dim(owner_local, my_block * TPB, TPB)
    own_rank = lax.dynamic_slice_in_dim(pair_rank, my_block * TPB, TPB)
    packed = jnp.concatenate([dycore_air_mass[:, None], dycore_face_flux], axis=1)
    lower = jnp.where(is_mine, block_col * PEER + pair_rank, -1)
    upper = jnp.where(is_mine, (column_count + block_col) * PEER + pair_rank, -1)
    spread = route_rows(lower, group_count * PEER) + route_rows(upper, group_count * PEER)
    weights = jnp.dot(spread, slot_hot, precision=highest)
    outgoing = jnp.einsum("rs,sctw->rctw", weights, packed, precision=highest)
    outgoing = outgoing.reshape(group_count, PEER, 3, band_rows, cells_y)
    incoming = lax.all_to_all(outgoing, ("grp", "gy"), split_axis=0, concat_axis=0, tiled=True)
    received = incoming.reshape(group_count * PEER, 3, band_rows, cells_y)
    pieces = jnp.take(received, own_local * PEER + own_rank, axis=0)
    cells_x = TPB * band_rows
    air_mass = pieces[:, 0].reshape(cells_x, cells_y)
    flows = (
        jnp.stack([pieces[:, 1].reshape(cells_x, cells_y), pieces[:, 2].reshape(cells_x, cells_y)])
        / NSUB
    )
    local_count = tracers.shape[0]
    stacked = jnp.concatenate([tracers, flows], axis=0)
    padded_all = extended(stacked, (("gx", 1), ("gy", 2)), 2)
    flow_x_pad = padded_all[local_count]
    flow_y_pad = padded_all[local_count + 1]
    padded = padded_all[:local_count]
    mixing = tracers
    for substep in range(NSUB):
        if substep > 0:
            padded = extended(mixing, (("gx", 1), ("gy", 2)), 2)
        mass_next = mass_update(flow_x_pad, flow_y_pad, air_mass)
        mixing = advance(padded, flow_x_pad, flow_y_pad, air_mass, mass_next)
        air_mass = mass_next
    local_index = water_idx - my_half * local_count
    held = (local_index >= 0) & (local_index < local_count)
    water_tracers = jnp.take(mixing, jnp.clip(local_index, 0, local_count - 1), axis=0)
    water_tracers = jnp.where(held[:, None, None], water_tracers, 0.0)
    water_pieces = water_tracers.reshape(-1, TPB, band_rows, cells_y).transpose(1, 0, 2, 3)
    to_owner = route_rows(own_local * PEER + own_rank, group_count * PEER)
    outgoing = jnp.einsum("rj,jctw->rctw", to_owner, water_pieces, precision=highest)
    outgoing = outgoing.reshape(group_count, PEER, -1, band_rows, cells_y)
    incoming = lax.all_to_all(outgoing, ("grp", "gy"), split_axis=0, concat_axis=0, tiled=True)
    received = incoming.reshape(group_count * PEER, -1, band_rows, cells_y)
    collect = jnp.dot(slot_hot.T, spread.T, precision=highest)
    water_to_dycore = jnp.einsum("sr,rctw->sctw", collect, received, precision=highest)
    return (mixing, water_to_dycore)


def solution(mesh):
    return jax.shard_map(
        per_device,
        mesh=mesh,
        in_specs=(
            P("grp", "gx", "gy"),
            P(("grp", "gx", "gy"), None, None),
            P(("grp", "gx", "gy"), None, None, None),
            P(),
            P(),
        ),
        out_specs=(P("grp", "gx", "gy"), P(("grp", "gx", "gy"), None, None, None)),
        check_vma=False,
    )
```

profile of v0, /device:TPU:96, one launch (start us, length us, event | category | flops | bytes accessed | tf_op | source)
XLA Modules:
  0.0 415.2 jit_solution(13175222803034287283)
XLA Ops:
  0.6 0.7 fusion.59
  1.9 1.1 copy.37
  3.0 0.9 copy.67
  4.2 0.8 convolution_bitcast_fusion.1
  5.0 0.9 copy.38
  6.0 4.3 %all-to-all-start = ((f32[8,1,3,16,384]{4,3,2,1,0:T(8,128)}), f32[8,1,3,16,384]{4,3,2,1,0:T(8,128)S(1)}, u32[]{:S(2)}, u32[]{:S(2)}) async-start(f32[8,1,3,16,384]{4,3,2,1,0:T(8,128)} %copy.38), calls=%async_computation | async-start | bytes 1179648 | tf_op jit(solution)/shard_map/all_to_all | solution.py:107
  10.9 10.4 %all-to-all-done = f32[8,1,3,16,384]{4,3,2,1,0:T(8,128)S(1)} async-done(((f32[8,1,3,16,384]{4,3,2,1,0:T(8,128)}), f32[8,1,3,16,384]{4,3,2,1,0:T(8,128)S(1)}, u32[]{:S(2)}, u32[]{:S(2)}) %all-to-all-start) | async-done | bytes 589856 | tf_op jit(solution)/shard_map/all_to_all | solution.py:107
  22.0 2.3 pad_maximum_fusion.13
  24.4 5.0 %collective-permute-start.1 = (f32[130,2,384]{2,1,0:T(2,128)S(1)}, f32[130,2,384]{2,1,0:T(2,128)S(1)}, u32[]{:S(2)}, u32[]{:S(2)}) collective-permute-start(f32[130,2,384]{2,1,0:T(2,128)S(1)} %get-tuple-element.33), channel_id=1, source_target_pairs={{4,0},{8,4},{12,8},{16,12},{20,16},{24,20},{28,24},{32,28},{36,32}... | collective-permute-start | bytes 1198088 | tf_op jit(solution)/shard_map/ppermute | solution.py:19
  29.4 1.9 collective-permute-start
  31.3 6.3 %collective-permute-done.1 = f32[130,2,384]{2,1,0:T(2,128)S(1)} collective-permute-done((f32[130,2,384]{2,1,0:T(2,128)S(1)}, f32[130,2,384]{2,1,0:T(2,128)S(1)}, u32[]{:S(2)}, u32[]{:S(2)}) %collective-permute-start.1) | collective-permute-done | bytes 399392 | tf_op jit(solution)/shard_map/ppermute | solution.py:19
  37.6 6.2 %collective-permute-done = f32[130,2,384]{2,1,0:T(2,128)S(1)} collective-permute-done((f32[130,2,384]{2,1,0:T(2,128)S(1)}, f32[130,2,384]{2,1,0:T(2,128)S(1)}, u32[]{:S(2)}, u32[]{:S(2)}) %collective-permute-start) | collective-permute-done | bytes 399392 | tf_op jit(solution)/shard_map/ppermute | solution.py:16
  43.8 6.8 %pad_maximum_fusion.8 = (f32[130,68,2]{2,1,0:T(8,128)}, f32[130,68,2]{2,1,0:T(8,128)}) fusion(f32[130,2,384]{2,1,0:T(2,128)S(1)} %collective-permute-done.1, f32[130,2,384]{2,1,0:T(2,128)S(1)} %collective-permute-done, f32[2,64,384]{2,1,0:T(8,128)S(1)} %maximum_multiply_fusion, f32[128,64,384]{2,1,0:T(8,128)S(1)} %copy-done), kind=kLoop, calls=%fused_computation.56 | loop fusion | flops 106080 | bytes 13719680 | tf_op jit(solution)/shard_map/slice | solution.py:17
  50.6 3.3 copy.39
  53.9 1.3 collective-permute-start.2
  55.2 3.3 copy.40
  58.5 1.6 collective-permute-start.3
  60.1 20.0 %maximum_maximum_fusion.2 = (f32[130,66,384]{2,1,0:T(8,128)}, f32[130,66,384]{2,1,0:T(8,128)}) fusion(f32[2,64,384]{2,1,0:T(8,128)S(1)} %maximum_multiply_fusion, f32[128,64,384]{2,1,0:T(8,128)} %param.5, f32[130,2,384]{2,1,0:T(2,128)S(1)} %collective-permute-done, f32[130,2,384]{2,1,0:T(2,128)S(1)} %collective-permute-done.1), kind=kLoop, calls=%fused_computation.22 | loop fusion | flops 13178880 | bytes 39936000 | tf_op jit(solution)/shard_map/concatenate | solution.py:20
  80.2 3.1 copy.41
  83.3 3.1 copy.42
  86.5 1.2 maximum_bitcast_fusion
  88.7 31.8 %maximum_maximum_fusion = (f32[130,68,386]{2,1,0:T(8,128)}, f32[130,68,386]{2,1,0:T(8,128)}) fusion(f32[130,2,384]{2,1,0:T(2,128)S(1)} %collective-permute-done.1, f32[2,64,384]{2,1,0:T(8,128)S(1)} %maximum_multiply_fusion, f32[128,64,384]{2,1,0:T(8,128)} %param.5, f32[130,2,384]{2,1,0:T(2,128)S(1)} %collective-permute-done, f32[130,68,2]{2,1,0:T(8,128)S(1)} %bitcast.40, ...), kind=kLoop, calls=%fused_computation.2 | loop fusion | flops 27297920 | bytes 41017600 | tf_op jit(solution)/shard_map/concatenate | solution.py:20
  120.5 39.4 %fusion.8 = f32[128,64,385]{2,1,0:T(8,128)} fusion(f32[130,68,386]{2,1,0:T(8,128)} %get-tuple-element.23, f32[130,68,386]{2,1,0:T(8,128)} %get-tuple-element.22, f32[64,385]{1,0:T(8,128)S(1)} %slice.244, pred[64,385]{1,0:T(8,128)(4,1)S(1)} %broadcast_compare_fusion), kind=kLoop, calls=%fused_computation.17 | loop fusion | flops 41000960 | bytes 63201600 | tf_op jit(solution)/shard_map/mul | solution.py:27
  159.9 27.4 %fusion.21 = f32[128,65,384]{2,1,0:T(8,128)} fusion(f32[130,66,384]{2,1,0:T(8,128)} %get-tuple-element.31, f32[130,66,384]{2,1,0:T(8,128)} %get-tuple-element.30, f32[65,384]{1,0:T(8,128)S(1)} %slice.237, pred[65,384]{1,0:T(8,128)(4,1)S(1)} %broadcast_compare_fusion.1), kind=kLoop, calls=%fused_computation.38 | loop fusion | flops 41533440 | bytes 64022400 | tf_op jit(solution)/shard_map/mul | solution.py:27
  187.3 27.7 %fusion.29 = f32[128,64,384]{2,1,0:T(8,128)} fusion(f32[128,64,385]{2,1,0:T(8,128)} %fusion.8, f32[128,65,384]{2,1,0:T(8,128)} %fusion.21, f32[128,64,384]{2,1,0:T(8,128)} %param.5, f32[64,384]{1,0:T(8,128)S(1)} %bitcast.43, f32[64,384]{1,0:T(8,128)S(1)} %get-tuple-element.13), kind=kLoop, calls=%fused_computation.50 | loop fusion | flops 18874368 | bytes 75694080 | tf_op jit(solution)/shard_map/div | solution.py:58
  215.0 2.2 fusion.65
  217.2 1.9 collective-permute-start.5
  219.1 3.9 collective-permute-start.4
  223.1 7.0 %collective-permute-done.5 = f32[128,2,384]{2,1,0:T(2,128)S(1)} collective-permute-done((f32[128,2,384]{2,1,0:T(2,128)S(1)}, f32[128,2,384]{2,1,0:T(2,128)S(1)}, u32[]{:S(2)}, u32[]{:S(2)}) %collective-permute-start.5) | collective-permute-done | bytes 393248 | tf_op jit(solution)/shard_map/ppermute | solution.py:19
  230.1 4.0 collective-permute-done.4
  234.1 7.0 %pad_maximum_fusion.11 = (f32[128,68,2]{2,1,0:T(8,128)}, f32[128,68,2]{2,1,0:T(8,128)}) fusion(f32[128,2,384]{2,1,0:T(2,128)S(1)} %collective-permute-done.5, f32[128,64,384]{2,1,0:T(8,128)} %fusion.29, f32[128,2,384]{2,1,0:T(2,128)S(1)} %collective-permute-done.4), kind=kLoop, calls=%fused_computation.59 | loop fusion | flops 69632 | bytes 13508608 | tf_op jit(solution)/shard_map/slice | solution.py:17
  241.2 3.5 copy.45
  244.7 2.7 collective-permute-start.6
  247.3 3.5 copy.47
  250.9 1.3 collective-permute-start.7
  252.2 26.8 %fusion.15 = f32[128,65,384]{2,1,0:T(8,128)} fusion(f32[128,2,384]{2,1,0:T(2,128)S(1)} %collective-permute-done.5, f32[128,64,384]{2,1,0:T(8,128)} %fusion.29, f32[128,2,384]{2,1,0:T(2,128)S(1)} %collective-permute-done.4, f32[65,384]{1,0:T(8,128)S(1)} %slice.237, pred[65,384]{1,0:T(8,128)(4,1)S(1)} %broadcast_compare_fusion.1), kind=kLoop, calls=%fused_computation.28 | loop fusion | flops 54312960 | bytes 26273664 | tf_op jit(solution)/shard_map/mul | solution.py:27
  279.0 3.2 copy.46
  282.2 3.2 copy.48
  285.4 29.3 %maximum_maximum_fusion.1 = (f32[128,68,386]{2,1,0:T(8,128)}, f32[128,68,386]{2,1,0:T(8,128)}) fusion(f32[128,2,384]{2,1,0:T(2,128)S(1)} %collective-permute-done.5, f32[128,64,384]{2,1,0:T(8,128)} %fusion.29, f32[128,2,384]{2,1,0:T(2,128)S(1)} %collective-permute-done.4, f32[128,68,2]{2,1,0:T(8,128)} %copy.46, f32[128,68,2]{2,1,0:T(8,128)} %copy.48), kind=kLoop, calls=%fused_computation.4 | loop fusion | flops 20158464 | bytes 40386560 | tf_op jit(solution)/shard_map/concatenate | solution.py:20
  314.7 39.3 %fusion.2 = f32[128,64,385]{2,1,0:T(8,128)} fusion(f32[128,68,386]{2,1,0:T(8,128)} %get-tuple-element.27, f32[128,68,386]{2,1,0:T(8,128)} %get-tuple-element.26, f32[64,385]{1,0:T(8,128)S(1)} %slice.244, pred[64,385]{1,0:T(8,128)(4,1)S(1)} %broadcast_compare_fusion), kind=kLoop, calls=%fused_computation.9 | loop fusion | flops 41000960 | bytes 63201600 | tf_op jit(solution)/shard_map/mul | solution.py:27
  354.0 27.9 %fusion.26 = f32[128,64,384]{2,1,0:T(8,128)} fusion(f32[128,64,385]{2,1,0:T(8,128)} %fusion.2, f32[128,65,384]{2,1,0:T(8,128)} %fusion.15, f32[128,64,384]{2,1,0:T(8,128)} %fusion.29, f32[64,384]{1,0:T(8,128)S(1)} %get-tuple-element.12, f32[64,384]{1,0:T(8,128)S(1)} %get-tuple-element.13), kind=kLoop, calls=%fused_computation.45 | loop fusion | flops 18874368 | bytes 75694080 | tf_op jit(solution)/shard_map/div | solution.py:58
  381.9 5.2 %gather_fusion.1 = f32[6,64,384]{2,1,0:T(8,128)S(1)} fusion(f32[128,64,384]{2,1,0:T(8,128)} %fusion.26, s32[1024]{0:T(1024)S(1)} %pad_clamp_fusion), kind=kCustom, calls=%fused_computation.1 | custom fusion | bytes 1179672 | tf_op jit(solution)/shard_map/jit(_take)/gather | solution.py:131
  387.1 1.0 convolution_bitcast_fusion
  388.1 1.3 copy.50
  389.4 5.8 %all-to-all-start.1 = ((f32[8,1,6,16,384]{4,3,2,1,0:T(8,128)}), f32[8,1,6,16,384]{4,3,2,1,0:T(8,128)S(1)}, u32[]{:S(2)}, u32[]{:S(2)}) async-start(f32[8,1,6,16,384]{4,3,2,1,0:T(8,128)} %copy.50), calls=%async_computation.1 | async-start | bytes 2359296 | tf_op jit(solution)/shard_map/all_to_all | solution.py:137
  395.5 17.0 %all-to-all-done.1 = f32[8,1,6,16,384]{4,3,2,1,0:T(8,128)S(1)} async-done(((f32[8,1,6,16,384]{4,3,2,1,0:T(8,128)}), f32[8,1,6,16,384]{4,3,2,1,0:T(8,128)S(1)}, u32[]{:S(2)}, u32[]{:S(2)}) %all-to-all-start.1) | async-done | bytes 1179680 | tf_op jit(solution)/shard_map/all_to_all | solution.py:137
  412.5 1.7 fusion.31
  414.1 0.9 copy.52
  (57 shorter events, 3.6 us)
Async XLA Ops:
  1.3 4.6 %copy-start.7 = (s32[256]{0:T(256)}, s32[256]{0:T(256)S(1)}, u32[]{:S(2)}) copy-start(s32[256]{0:T(256)S(1)} %get-tuple-element.39) | copy-start | bytes 3076
  1.9 4.1 copy-start.3
  1.9 4.1 copy-start.9
  1.9 4.1 copy-start.5
  6.0 15.3 %all-to-all-start = ((f32[8,1,3,16,384]{4,3,2,1,0:T(8,128)}), f32[8,1,3,16,384]{4,3,2,1,0:T(8,128)S(1)}, u32[]{:S(2)}, u32[]{:S(2)}) async-start(f32[8,1,3,16,384]{4,3,2,1,0:T(8,128)} %copy.38), calls=%async_computation | async-start | bytes 1179648 | tf_op jit(solution)/shard_map/all_to_all | solution.py:107
  10.4 0.5 copy-start.1
  21.9 21.9 %copy-start = (f32[128,64,384]{2,1,0:T(8,128)S(1)}, f32[128,64,384]{2,1,0:T(8,128)}, u32[]{:S(2)}) copy-start(f32[128,64,384]{2,1,0:T(8,128)} %param.5) | copy-start | bytes 37748740
  24.4 13.2 %collective-permute-start.1 = (f32[130,2,384]{2,1,0:T(2,128)S(1)}, f32[130,2,384]{2,1,0:T(2,128)S(1)}, u32[]{:S(2)}, u32[]{:S(2)}) collective-permute-start(f32[130,2,384]{2,1,0:T(2,128)S(1)} %get-tuple-element.33), channel_id=1, source_target_pairs={{4,0},{8,4},{12,8},{16,12},{20,16},{24,20},{28,24},{32,28},{36,32}... | collective-permute-start | bytes 1198088 | tf_op jit(solution)/shard_map/ppermute | solution.py:19
  29.4 14.4 %collective-permute-start = (f32[130,2,384]{2,1,0:T(2,128)S(1)}, f32[130,2,384]{2,1,0:T(2,128)S(1)}, u32[]{:S(2)}, u32[]{:S(2)}) collective-permute-start(f32[130,2,384]{2,1,0:T(2,128)S(1)} %get-tuple-element.32), channel_id=1, source_target_pairs={{0,4},{4,8},{8,12},{12,16},{16,20},{20,24},{24,28},{28,32},{32,36}... | collective-permute-start | bytes 1198088 | tf_op jit(solution)/shard_map/ppermute | solution.py:16
  53.9 26.2 %collective-permute-start.2 = (f32[130,68,2]{1,2,0:T(2,128)S(1)}, f32[130,68,2]{1,2,0:T(2,128)S(1)}, u32[]{:S(2)}, u32[]{:S(2)}) collective-permute-start(f32[130,68,2]{1,2,0:T(2,128)S(1)} %copy.39), channel_id=1, source_target_pairs={{0,1},{1,2},{2,3},{4,5},{5,6},{6,7},{8,9},{9,10},{10,11},{12,13},{... | collective-permute-start | bytes 212168 | tf_op jit(solution)/shard_map/ppermute | solution.py:16
  58.5 24.8 %collective-permute-start.3 = (f32[130,68,2]{1,2,0:T(2,128)S(1)}, f32[130,68,2]{1,2,0:T(2,128)S(1)}, u32[]{:S(2)}, u32[]{:S(2)}) collective-permute-start(f32[130,68,2]{1,2,0:T(2,128)S(1)} %copy.40), channel_id=1, source_target_pairs={{1,0},{2,1},{3,2},{5,4},{6,5},{7,6},{9,8},{10,9},{11,10},{13,12},{... | collective-permute-start | bytes 212168 | tf_op jit(solution)/shard_map/ppermute | solution.py:19
  83.3 4.9 %slice-start = ((s8[4792320]{0:T(1024)(128)(4,1)}), s8[598016]{0:T(1024)(128)(4,1)S(1)}, s32[]{:S(2)}) async-start(s8[4792320]{0:T(1024)(128)(4,1)} %bitcast.39), calls=%async_computation.2 | async-start | bytes 1196032
  86.5 2.3 slice-start.1
  187.3 35.7 %copy-start.11 = (s32[6]{0:T(128)S(1)}, s32[6]{0:T(128)}, u32[]{:S(2)}) copy-start(s32[6]{0:T(128)} %param.9) | copy-start | bytes 76
  217.2 12.9 %collective-permute-start.5 = (f32[128,2,384]{2,1,0:T(2,128)S(1)}, f32[128,2,384]{2,1,0:T(2,128)S(1)}, u32[]{:S(2)}, u32[]{:S(2)}) collective-permute-start(f32[128,2,384]{2,1,0:T(2,128)S(1)} %get-tuple-element.35), channel_id=1, source_target_pairs={{4,0},{8,4},{12,8},{16,12},{20,16},{24,20},{28,24},{32,28},{36,32}... | collective-permute-start | bytes 1179656 | tf_op jit(solution)/shard_map/ppermute | solution.py:19
  219.1 15.0 %collective-permute-start.4 = (f32[128,2,384]{2,1,0:T(2,128)S(1)}, f32[128,2,384]{2,1,0:T(2,128)S(1)}, u32[]{:S(2)}, u32[]{:S(2)}) collective-permute-start(f32[128,2,384]{2,1,0:T(2,128)S(1)} %get-tuple-element.34), channel_id=1, source_target_pairs={{0,4},{4,8},{8,12},{12,16},{16,20},{20,24},{24,28},{28,32},{32,36}... | collective-permute-start | bytes 1179656 | tf_op jit(solution)/shard_map/ppermute | solution.py:16
  244.7 34.3 %collective-permute-start.6 = (f32[128,68,2]{0,2,1:T(2,128)S(1)}, f32[128,68,2]{0,2,1:T(2,128)S(1)}, u32[]{:S(2)}, u32[]{:S(2)}) collective-permute-start(f32[128,68,2]{0,2,1:T(2,128)S(1)} %copy.45), channel_id=1, source_target_pairs={{0,1},{1,2},{2,3},{4,5},{5,6},{6,7},{8,9},{9,10},{10,11},{12,13},{... | collective-permute-start | bytes 208904 | tf_op jit(solution)/shard_map/ppermute | solution.py:16
  250.9 31.3 %collective-permute-start.7 = (f32[128,68,2]{0,2,1:T(2,128)S(1)}, f32[128,68,2]{0,2,1:T(2,128)S(1)}, u32[]{:S(2)}, u32[]{:S(2)}) collective-permute-start(f32[128,68,2]{0,2,1:T(2,128)S(1)} %copy.47), channel_id=1, source_target_pairs={{1,0},{2,1},{3,2},{5,4},{6,5},{7,6},{9,8},{10,9},{11,10},{13,12},{... | collective-permute-start | bytes 208904 | tf_op jit(solution)/shard_map/ppermute | solution.py:19
  354.0 33.1 %copy-start.2 = (s32[4]{0:T(128)S(1)}, s32[4]{0:T(128)}, u32[]{:S(2)}) copy-start(s32[4]{0:T(128)} %copy-done.1) | copy-start | bytes 52
  354.0 41.2 %copy-start.4 = (pred[256]{0:T(512)(128)(4,1)S(1)}, pred[256]{0:T(512)(128)(4,1)}, u32[]{:S(2)}) copy-start(pred[256]{0:T(512)(128)(4,1)} %copy-done.3) | copy-start | bytes 772
  354.0 41.2 %copy-start.6 = (s32[256]{0:T(256)S(1)}, s32[256]{0:T(256)}, u32[]{:S(2)}) copy-start(s32[256]{0:T(256)} %copy-done.5) | copy-start | bytes 3076
  354.0 41.2 %copy-start.8 = (s32[256]{0:T(256)S(1)}, s32[256]{0:T(256)}, u32[]{:S(2)}) copy-start(s32[256]{0:T(256)} %copy-done.7) | copy-start | bytes 3076
  354.0 41.2 %copy-start.10 = (s32[256]{0:T(256)S(1)}, s32[256]{0:T(256)}, u32[]{:S(2)}) copy-start(s32[256]{0:T(256)} %copy-done.9) | copy-start | bytes 3076
  389.4 23.1 %all-to-all-start.1 = ((f32[8,1,6,16,384]{4,3,2,1,0:T(8,128)}), f32[8,1,6,16,384]{4,3,2,1,0:T(8,128)S(1)}, u32[]{:S(2)}, u32[]{:S(2)}) async-start(f32[8,1,6,16,384]{4,3,2,1,0:T(8,128)} %copy.50), calls=%async_computation.1 | async-start | bytes 2359296 | tf_op jit(solution)/shard_map/all_to_all | solution.py:137
where the time goes:
time: 420 us; the launch traced here: 415 us
  other arithmetic  288 us (69%)
  waiting for transfers between devices  51 us (12%)
  local copies, waits for them, and re-layouts  40.8 us (10%)
  starting transfers between devices  29.7 us (7%)
    mul x4, other arithmetic, upwind_faces(): return flow * jnp.where(flow > 0, from_left, from_right)  133 us
    concatenate x3, other arithmetic, extended(): block = jnp.concatenate([low, block, high], axis=dim)  81.2 us
    div x2, other arithmetic, advance(): (air_mass * centre - (flux_x[:, 1:] - flux_x[:, :-1]) - (flux_y[:, :, 1:]...  55.6 us
    all_to_all x2, waiting for transfers between devices, per_device(): lax.all_to_all(outgoing, ('grp', 'gy'), split_axis=0, concat_axis=0, tile...  27.4 us
    slice x3, other arithmetic, extended(): lax.slice_in_dim(block, block.shape[dim] - width, None, axis=dim)  16.2 us
    ppermute x4, waiting for transfers between devices, extended(): lax.ppermute(lax.slice_in_dim(block, 0, width, axis=dim), axis, backward)  13.3 us
    ppermute x4, waiting for transfers between devices, extended(): lax.ppermute(lax.slice_in_dim(block, block.shape[dim] - width, None, axis...  10.3 us
    all_to_all x2, starting transfers between devices, per_device(): lax.all_to_all(outgoing, ('grp', 'gy'), split_axis=0, concat_axis=0, tile...  10.1 us
  transfers between devices with their start and end apart: 10, of which 6 were waited for; matrix products, arithmetic and copies ran while one was open for 15% of the time, Pallas kernels for 0%

commit v1 on v0

v1 whole, which is shorter than its diff:
```python
import jax
import jax.numpy as jnp
import numpy as np
from jax import lax
from jax.experimental import pallas as pl
from jax.experimental.pallas import tpu as pltpu
from jax.sharding import PartitionSpec as P

MESH = pl.DeviceIdType.MESH
f32 = jnp.float32
bf16 = jnp.bfloat16

NG, NX, NY = 2, 16, 4
GROUP = NG * NY
TPB = 4
SLOTS = 4
ROWS = 16
J = 3
T = 8
NT = 128
CH = NT // T
NW = 6
PW = 5
EDGE = T * J * 2


def stencil_weights():
    w = np.zeros((256, 256), np.float32)
    for b, taps in enumerate(({-1: -1, 0: 5, 1: 2}, {0: 2, 1: 5, 2: -1})):
        for n in range(128):
            for d, v in taps.items():
                y = n + d
                if 0 <= y < 128:
                    w[y, b * 128 + n] += v
                    if 2 <= y < 126:
                        w[128 + y, b * 128 + n] += v
                else:
                    w[(256 + y) if y < 0 else y, b * 128 + n] += v
    return w


def lanes():
    return lax.broadcasted_iota(jnp.int32, (8, 128), 1)


def cat(a, b):
    return jnp.concatenate([a, b], 0)


def place(t, xg):
    return 4 * ((t % 4) * 8 + xg)


def pack_edges(old, t, xg, first, last):
    m = place(t, xg)
    lane = lanes()
    mixed = pltpu.roll(jnp.where(lane < 64, first, last), (m + 2) % 128, 1)
    return jnp.where((lane >> 2) == m // 4, mixed, old)


def merge_edges(left, right):
    return jnp.where((lanes() & 3) < 2, left, right)


def left_faces(left, own, flow):
    y = merge_edges(left, own)
    y1, y2, y3 = pltpu.roll(y, 1, 1), pltpu.roll(y, 2, 1), pltpu.roll(y, 3, 1)
    return flow * jnp.where(flow > 0, 5.0 * y2 + (2.0 * y1 - y3), 2.0 * y2 + (5.0 * y1 - y))


def advance(q, cf, sub, w, edges, faces, put, count, packed):
    lane16 = lax.broadcasted_iota(jnp.int32, (16, 128), 1)
    lane = lanes()
    half16 = lane16 < 64
    edge16 = (lane16 < 2) | (lane16 >= 126)
    main, second = [], []
    for xg in range(8):
        for t in range(0, count, 2):
            ts = [t, min(t + 1, count - 1)]
            av = [cat(*[q(u, j, 8 * xg) for u in ts]) for j in range(J)]
            uv = cat(*[pltpu.roll(edges[u // 4], (254 - place(u, xg)) % 128, 1) for u in ts]).astype(bf16)
            high = [a.astype(bf16) for a in av]
            for j in range(J):
                left = uv if j == 0 else high[j - 1]
                right = uv if j == J - 1 else high[j + 1]
                low = (av[j] - high[j].astype(f32)).astype(bf16)
                main.append(high[j])
                second.append(jnp.where(edge16, jnp.where(half16, right, left), low))
    lhs = jnp.concatenate([jnp.concatenate(main, 0), jnp.concatenate(second, 0)], 1)
    both = jnp.dot(lhs, w, preferred_element_type=f32)
    row = 0
    for xg in range(8):
        for t in range(0, count, 2):
            for u in range(2):
                if t + u >= count:
                    continue
                flux, moved = [], []
                for j in range(J):
                    r = slice((row + j) * 16 + u * 8, (row + j) * 16 + u * 8 + 8)
                    f = cf[j, xg, 4]
                    flux.append(f * jnp.where(f > 0, both[r, :128], both[r, 128:]))
                    moved.append(pltpu.roll(flux[j], 1, 1))
                before = pltpu.roll(faces[(t + u) // 4], (253 - place(t + u, xg)) % 128, 1)
                new = []
                for j in range(J):
                    x = [q(t + u, j, 8 * xg + d) for d in (-2, -1, 0, 1, 2)]
                    c = [cf[j, xg, k] for k in range(4)]
                    s = (c[0] * x[0] + c[1] * x[1]) + (c[2] * x[3] + c[3] * x[4])
                    v = cf[j, xg, 5 + 2 * sub] * x[2] - flux[j]
                    v = v + jnp.where(lane == 0, before if j == 0 else moved[j - 1], moved[j])
                    new.append((s + v) * cf[j, xg, 6 + 2 * sub])
                    put(t + u, j, xg, new[j])
                if packed is not None:
                    k = (t + u) // 4
                    packed[k] = pack_edges(packed[k], t + u, xg, new[0], new[J - 1])
            row += J
    return packed


def total(items):
    out = items[0]
    for item in items[1:]:
        out = out + item
    return out


def flag(condition):
    return jnp.where(condition, 1, 0).astype(jnp.int32)


def water_places(water_ref):
    ids = [water_ref[w] for w in range(NW)]
    halves = [i // NT for i in ids]
    ranks = [total([jnp.int32(0)] + [flag(halves[v] == halves[w]) for v in range(w)]) for w in range(NW)]
    ranks = [jnp.minimum(r, PW - 1) for r in ranks]
    return ids, halves, ranks


def first_kernel(
    slot_ref, water_ref, mass_ref, flux_ref, w_ref, tracers,
    q1, cf, lo2, hi2, zl2, zr2, z1, gpk, arrived,
    q0, q1v, up1, dn1, lo1, hi1, z0, zl1, zr1, up2, dn2, tsend, trecv, xsend, xrecv,
    mass, fx, fy, qw, qw1, upw, dnw, low, hiw, zw, zlw, zrw, q2w, wsend,
    load_sem, tile_ssem, tile_rsem, row_ssem, row_rsem, halo_ssem, halo_rsem,
    next_ssem, next_rsem, wh_ssem, wh_rsem, ws_sem, wr_sem, out_sem,
):
    grp, gx, gy = lax.axis_index("grp"), lax.axis_index("gx"), lax.axis_index("gy")
    me = (grp * NX + gx) * NY + gy
    pos = grp * NY + gy
    lane = lanes()

    def at(x, p):
        return {"grp": p // NY, "gx": x, "gy": lax.rem(p, NY)}

    def peer(k):
        return lax.rem(pos + k, GROUP)

    def load(c, j):
        return pltpu.make_async_copy(
            tracers.at[pl.ds(c * T, T), :, pl.ds(128 * j, 128)],
            q0.at[pl.ds(c * T, T), j, pl.ds(8, 64), :],
            load_sem.at[c, j],
        )

    def start_load(c, _):
        for j in range(J):
            load(c, j).start()
        return 0

    lax.fori_loop(0, CH, start_load, 0)

    barrier = pltpu.get_barrier_semaphore()

    def greet(device):
        pl.semaphore_signal(barrier, inc=1, device_id=device, device_id_type=MESH)

    for k in range(1, GROUP):
        greet(at(gx, peer(k)))

    @pl.when(gx > 0)
    def _():
        for k in range(GROUP):
            greet(at(gx - 1, peer(k)))

    @pl.when(gx < NX - 1)
    def _():
        for k in range(GROUP):
            greet(at(gx + 1, peer(k)))

    def held(c, only=None):
        choice = jnp.int32(0)
        for i in range(TPB) if only is None else (only,):
            g = slot_ref[(gx * NY + c) * TPB + i]
            choice = jnp.where(g // SLOTS == me, g % SLOTS, choice)
        return choice

    for c in range(NY):
        s = held(c)
        for j in range(J):
            cols = slice(128 * j, 128 * j + 128)
            tsend[c, pl.ds(16 * j, 16), :] = mass_ref[s, :, cols]
            tsend[c, pl.ds(48 + 16 * j, 16), :] = flux_ref[s, 0, :, cols]
            tsend[c, pl.ds(96 + 16 * j, 16), :] = flux_ref[s, 1, :, cols]
        if c > 0:
            b = held(c - 1)
            above = pltpu.roll(flux_ref[b, 1, pl.ds(8, 8), 256:384], 64, 1)
            tsend[c, pl.ds(144, 8), :] = jnp.where(lane < 64, above, flux_ref[b, 1, pl.ds(0, 8), 256:384])
        else:
            tsend[c, pl.ds(144, 8), :] = jnp.zeros((8, 128), f32)
        d = held(c, TPB - 1)
        xsend[c] = jnp.zeros((8, 128), f32)
        for j in range(J):
            xsend[c, pl.ds(j, 1), :] = flux_ref[d, 0, pl.ds(ROWS - 1, 1), 128 * j : 128 * j + 128]
    trecv[0] = tsend[gy]

    pl.semaphore_wait(barrier, GROUP - 1 + jnp.where(gx > 0, GROUP, 0) + jnp.where(gx < NX - 1, GROUP, 0))

    def tile_copy(k):
        return pltpu.make_async_remote_copy(
            src_ref=tsend.at[lax.rem(peer(k), NY)],
            dst_ref=trecv.at[k],
            send_sem=tile_ssem.at[k],
            recv_sem=tile_rsem.at[k],
            device_id=at(gx, peer(k)),
            device_id_type=MESH,
        )

    def row_copy(k):
        return pltpu.make_async_remote_copy(
            src_ref=xsend.at[lax.rem(peer(k), NY)],
            dst_ref=xrecv.at[k],
            send_sem=row_ssem.at[k],
            recv_sem=row_rsem.at[k],
            device_id=at(gx + 1, peer(k)),
            device_id_type=MESH,
        )

    for k in range(1, GROUP):
        tile_copy(k).start()

    @pl.when(gx < NX - 1)
    def _():
        for k in range(GROUP):
            row_copy(k).start()

    has = (gx < NX - 1, gx > 0, gy < NY - 1, gy > 0)
    get = (gx > 0, gx < NX - 1, gy > 0, gy < NY - 1)
    to = ({"gx": gx + 1}, {"gx": gx - 1}, {"gy": gy + 1}, {"gy": gy - 1})
    to = tuple({"grp": grp, "gx": gx, "gy": gy, **d} for d in to)

    def halo(d, src, dst, ssem, rsem):
        return pltpu.make_async_remote_copy(
            src_ref=src, dst_ref=dst, send_sem=ssem.at[d], recv_sem=rsem.at[d], device_id=to[d], device_id_type=MESH
        )

    sets1 = ((dn1, lo1), (up1, hi1), (z0, zl1), (z0, zr1))
    sets2 = ((dn2, lo2), (up2, hi2), (z1, zl2), (z1, zr2))
    setsw = ((dnw, low), (upw, hiw), (zw, zlw), (zw, zrw))

    def send_chunk(sets, c, ssem, rsem):
        for d, (src, dst) in enumerate(sets):

            @pl.when(has[d])
            def _(d=d, src=src, dst=dst):
                halo(d, src.at[c], dst.at[c], ssem, rsem).start()

    def wait_sets(sets, ssem, rsem, receive):
        for d, (src, dst) in enumerate(sets):
            copy = halo(d, src, dst, ssem, rsem)

            @pl.when(get[d] if receive else has[d])
            def _(copy=copy):
                (copy.wait_recv if receive else copy.wait_send)()

    def edge_rows(row):
        return [(t, j, (t * J + j) * 2) for t in range(row) for j in range(J)]

    def prepare(c, source, count):
        packed = [jnp.zeros((8, 128), f32)] * 2
        for t in range(count):
            for xg in range(8):
                packed[t // 4] = pack_edges(packed[t // 4], t, xg, source(t, 0, 8 * xg, 8), source(t, J - 1, 8 * xg, 8))
        for k in range(2):
            z0[c, k] = packed[k]
        for t, j, r in edge_rows(count):
            up1[c, pl.ds(r, 2), :] = source(t, j, 0, 2)
            dn1[c, pl.ds(r, 2), :] = source(t, j, 62, 2)
        send_chunk(sets1, c, halo_ssem, halo_rsem)

    def prepare_chunk(c, _):
        for j in range(J):
            load(c, j).wait()
        prepare(c, lambda t, j, r, n: q0[c * T + t, j, pl.ds(8 + r, n), :], T)
        return 0

    lax.fori_loop(0, CH, prepare_chunk, 0)

    ids, halves, ranks = water_places(water_ref)
    for p in range(PW):
        tracer = jnp.int32(0)
        for w in range(NW):
            tracer = jnp.where((halves[w] == grp) & (ranks[w] == p), ids[w] % NT, tracer)
        for j in range(J):
            qw[p, j, pl.ds(8, 64), :] = q0[tracer, j, pl.ds(8, 64), :]
    prepare(CH, lambda t, j, r, n: qw[t, j, pl.ds(8 + r, n), :], PW)

    for k in range(1, GROUP):
        tile_copy(k).wait_recv()

    @pl.when(gx > 0)
    def _():
        for k in range(GROUP):
            row_copy(k).wait_recv()

    def sender(tile):
        owner = slot_ref[tile] // SLOTS
        return lax.rem(pos + GROUP - (owner // (NX * NY) * NY + owner % NY), GROUP)

    base = (gx * NY + gy) * TPB
    left = []
    for i in range(TPB):
        k = sender(base + i)
        for j in range(J):
            mass[j, pl.ds(16 * i, 16), :] = trecv[k, pl.ds(16 * j, 16), :]
            fx[j, pl.ds(8 + 16 * i, 16), :] = trecv[k, pl.ds(48 + 16 * j, 16), :] * (1.0 / 12.0)
            fy[j, pl.ds(16 * i, 16), :] = trecv[k, pl.ds(96 + 16 * j, 16), :] * (1.0 / 12.0)
        k = sender(jnp.maximum(base - TPB, 0) + i)
        v = jnp.where(gy > 0, trecv[k, pl.ds(144, 8), :] * (1.0 / 12.0), 0.0)
        left += [v, pltpu.roll(v, 64, 1)]
    k = sender(jnp.maximum(base - NY * TPB, 0) + TPB - 1)
    for j in range(J):
        v = jnp.where(gx > 0, xrecv[k, pl.ds(j, 1), :] * (1.0 / 12.0), 0.0)
        fx[j, pl.ds(7, 1), :] = v
    g = jnp.zeros((8, 128), f32)
    for xg in range(8):
        g = jnp.where(lane == 4 * xg + 3, pltpu.roll(left[xg], 4 * xg + 4, 1), g)
    gpk[...] = (g + pltpu.roll(g, 32, 1)) + (pltpu.roll(g, 64, 1) + pltpu.roll(g, 96, 1))
    for xg in range(8):
        moved = []
        for j in range(J):
            f = fx[j, pl.ds(8 + 8 * xg, 8), :]
            b = fx[j, pl.ds(7 + 8 * xg, 8), :]
            fp, fm, gp, gm = jnp.maximum(f, 0.0), jnp.minimum(f, 0.0), jnp.maximum(b, 0.0), jnp.minimum(b, 0.0)
            h = fy[j, pl.ds(8 * xg, 8), :]
            moved.append(pltpu.roll(h, 1, 1))
            last = pltpu.roll(left[xg], 1, 1) if j == 0 else moved[j - 1]
            out = 6.0 * ((f - b) + (h - jnp.where(lane == 0, last, moved[j])))
            m0 = mass[j, pl.ds(8 * xg, 8), :]
            m1 = m0 - out
            m2 = m1 - out
            centre = (5.0 * fp + 2.0 * fm) - (2.0 * gp + 5.0 * gm)
            cf[j, xg, 0] = -gp
            cf[j, xg, 1] = fp + (5.0 * gp + 2.0 * gm)
            cf[j, xg, 2] = -(2.0 * fp + 5.0 * fm) - gm
            cf[j, xg, 3] = fm
            cf[j, xg, 4] = h
            cf[j, xg, 5] = m0 - centre
            cf[j, xg, 6] = 1.0 / m1
            cf[j, xg, 7] = m1 - centre
            cf[j, xg, 8] = 1.0 / m2

    wait_sets(sets1, halo_ssem, halo_rsem, True)

    def fill(dst, c, count, lo, hi):
        for t, j, r in edge_rows(count):
            dst(t, j, 6, jnp.where(get[0], lo[c, pl.ds(r, 2), :], 0.0))
            dst(t, j, 72, jnp.where(get[1], hi[c, pl.ds(r, 2), :], 0.0))

    def edge_terms(zl, zr, zo, c):
        zls = [jnp.where(get[2], zl[c, k], 0.0) for k in range(2)]
        zrs = [jnp.where(get[3], zr[c, k], 0.0) for k in range(2)]
        return [merge_edges(a, b) for a, b in zip(zls, zrs)], [left_faces(zls[k], zo[c, k], gpk[...]) for k in range(2)]

    def put_qw(t, j, r, v):
        qw[t, j, pl.ds(r, 2), :] = v

    fill(put_qw, CH, PW, lo1, hi1)
    edges, faces = edge_terms(zl1, zr1, z0, CH)

    def put_qw1(t, j, xg, v):
        qw1[t, j, pl.ds(8 + 8 * xg, 8), :] = v

    packed = advance(
        lambda t, j, r: qw[t, j, pl.ds(8 + r, 8), :], cf, 0, w_ref[...], edges, faces, put_qw1, PW,
        [jnp.zeros((8, 128), f32)] * 2,
    )
    for k in range(2):
        zw[0, k] = packed[k]
    for t, j, r in edge_rows(PW):
        upw[0, pl.ds(r, 2), :] = qw1[t, j, pl.ds(8, 2), :]
        dnw[0, pl.ds(r, 2), :] = qw1[t, j, pl.ds(70, 2), :]
    send_chunk(setsw, 0, wh_ssem, wh_rsem)

    def water_copy(k):
        return pltpu.make_async_remote_copy(
            src_ref=wsend.at[k],
            dst_ref=arrived.at[k],
            send_sem=ws_sem.at[k],
            recv_sem=wr_sem.at[k],
            device_id=at(gx, peer(k)),
            device_id_type=MESH,
        )

    def own_water():
        return pltpu.make_async_copy(wsend.at[0], arrived.at[0], ws_sem.at[0])

    def finish_water():
        wait_sets(setsw, wh_ssem, wh_rsem, True)

        def put_halo(t, j, r, v):
            qw1[t, j, pl.ds(r, 2), :] = v

        fill(put_halo, 0, PW, low, hiw)
        edges, faces = edge_terms(zlw, zrw, zw, 0)

        def put_q2(t, j, xg, v):
            q2w[xg // 2, t, j, pl.ds(8 * (xg % 2), 8), :] = v

        advance(
            lambda t, j, r: qw1[t, j, pl.ds(8 + r, 8), :], cf, 1, w_ref[...], edges, faces, put_q2, PW, None
        )
        for k in range(GROUP):
            p = peer(k)
            owners = [slot_ref[base + i] // SLOTS for i in range(TPB)]
            tile = jnp.int32(0)
            for i in range(TPB):
                tile = jnp.where(owners[i] // (NX * NY) * NY + owners[i] % NY == p, i, tile)
            wsend[k] = q2w[tile]
        own_water().start()
        for k in range(1, GROUP):
            water_copy(k).start()

    def out_copy(c):
        return pltpu.make_async_copy(q1v.at[pl.ds(c * T, T)], q1.at[pl.ds(c * T, T)], out_sem.at[0])

    def chunk(c, _):
        def put_q0(t, j, r, v):
            q0[c * T + t, j, pl.ds(r, 2), :] = v

        fill(put_q0, c, T, lo1, hi1)
        edges, faces = edge_terms(zl1, zr1, z0, c)

        def put_q1(t, j, xg, v):
            q1v[c * T + t, j, pl.ds(8 * xg, 8), :] = v

        packed = advance(
            lambda t, j, r: q0[c * T + t, j, pl.ds(8 + r, 8), :], cf, 0, w_ref[...], edges, faces, put_q1, T,
            [jnp.zeros((8, 128), f32)] * 2,
        )
        for k in range(2):
            z1[c, k] = packed[k]
        for t, j, r in edge_rows(T):
            up2[c, pl.ds(r, 2), :] = q1v[c * T + t, j, pl.ds(0, 2), :]
            dn2[c, pl.ds(r, 2), :] = q1v[c * T + t, j, pl.ds(62, 2), :]
        out_copy(c).start()
        send_chunk(sets2, c, next_ssem, next_rsem)

        @pl.when(c == 2)
        def _():
            finish_water()

        return 0

    lax.fori_loop(0, CH, chunk, 0)

    for k in range(1, GROUP):
        tile_copy(k).wait_send()

    @pl.when(gx < NX - 1)
    def _():
        for k in range(GROUP):
            row_copy(k).wait_send()

    wait_sets(sets1, halo_ssem, halo_rsem, False)
    wait_sets(setsw, wh_ssem, wh_rsem, False)
    wait_sets(sets2, next_ssem, next_rsem, False)
    wait_sets(sets2, next_ssem, next_rsem, True)
    pltpu.make_async_copy(q1v, q1, out_sem.at[0]).wait()
    own_water().wait()
    for k in range(1, GROUP):
        water_copy(k).wait()


def second_kernel(
    slot_ref, water_ref, w_ref, cf, lo, hi, zl, zr, zo, gpk, arrived, q1,
    out, water, qb, ob, in_sem, out_sem,
):
    grp, gx, gy = lax.axis_index("grp"), lax.axis_index("gx"), lax.axis_index("gy")
    me = (grp * NX + gx) * NY + gy
    pos = grp * NY + gy

    def load(c, s):
        return pltpu.make_async_copy(q1.at[pl.ds(c * T, T)], qb.at[s, :, :, pl.ds(8, 64), :], in_sem.at[s])

    def store(c, s, j):
        return pltpu.make_async_copy(
            ob.at[s, :, j], out.at[pl.ds(c * T, T), :, pl.ds(128 * j, 128)], out_sem.at[s, j]
        )

    load(0, 0).start()

    ids, halves, ranks = water_places(water_ref)
    for s in range(SLOTS):
        column, valid = jnp.int32(0), jnp.int32(0)
        for c in range(NY):
            for i in range(TPB):
                match = slot_ref[(gx * NY + c) * TPB + i] == me * SLOTS + s
                column = jnp.where(match, c, column)
                valid = jnp.where(match, 1, valid)
        for w in range(NW):
            k = lax.rem(pos + GROUP - (halves[w] * NY + column), GROUP)
            for j in range(J):
                water[s, w, :, 128 * j : 128 * j + 128] = jnp.where(valid > 0, arrived[k, ranks[w], j], 0.0)

    def chunk(c, _):
        s = lax.rem(c, 2)

        @pl.when(c + 1 < CH)
        def _():
            load(c + 1, 1 - s).start()

        load(c, s).wait()

        @pl.when(c >= 2)
        def _():
            for j in range(J):
                store(c - 2, s, j).wait()

        for t in range(T):
            for j in range(J):
                r = (t * J + j) * 2
                qb[s, t, j, pl.ds(6, 2), :] = jnp.where(gx > 0, lo[c, pl.ds(r, 2), :], 0.0)
                qb[s, t, j, pl.ds(72, 2), :] = jnp.where(gx < NX - 1, hi[c, pl.ds(r, 2), :], 0.0)
        zls = [jnp.where(gy > 0, zl[c, k], 0.0) for k in range(2)]
        zrs = [jnp.where(gy < NY - 1, zr[c, k], 0.0) for k in range(2)]
        edges = [merge_edges(a, b) for a, b in zip(zls, zrs)]
        faces = [left_faces(zls[k], zo[c, k], gpk[...]) for k in range(2)]

        def put(t, j, xg, v):
            ob[s, t, j, pl.ds(8 * xg, 8), :] = v

        advance(lambda t, j, r: qb[s, t, j, pl.ds(8 + r, 8), :], cf, 1, w_ref[...], edges, faces, put, T, None)
        for j in range(J):
            store(c, s, j).start()
        return 0

    lax.fori_loop(0, CH, chunk, 0)
    for c in (CH - 2, CH - 1):
        for j in range(J):
            store(c, c % 2, j).wait()


def per_device(tracers, dycore_air_mass, dycore_face_flux, tile_dycore_slot, water_idx):
    weights = jnp.asarray(stencil_weights(), bf16)
    smem = pl.BlockSpec(memory_space=pltpu.SMEM)
    vmem = pl.BlockSpec(memory_space=pltpu.VMEM)
    hbm = pl.BlockSpec(memory_space=pl.ANY)
    V, D = pltpu.VMEM, pltpu.SemaphoreType.DMA

    def S(*shape):
        return jax.ShapeDtypeStruct(shape, f32)

    edge, packs = (EDGE, 128), (2, 8, 128)
    scratch = [
        V((NT, J, 80, 128), f32), V((NT, J, 64, 128), f32),
        V((CH + 1, *edge), f32), V((CH + 1, *edge), f32), V((CH + 1, *edge), f32), V((CH + 1, *edge), f32),
        V((CH + 1, *packs), f32), V((CH + 1, *packs), f32), V((CH + 1, *packs), f32),
        V((CH, *edge), f32), V((CH, *edge), f32),
        V((NY, 152, 128), f32), V((GROUP, 152, 128), f32), V((NY, 8, 128), f32), V((GROUP, 8, 128), f32),
        V((J, 64, 128), f32), V((J, 72, 128), f32), V((J, 64, 128), f32),
        V((PW, J, 80, 128), f32), V((PW, J, 80, 128), f32),
        V((1, *edge), f32), V((1, *edge), f32), V((1, *edge), f32), V((1, *edge), f32),
        V((1, *packs), f32), V((1, *packs), f32), V((1, *packs), f32),
        V((TPB, PW, J, ROWS, 128), f32), V((GROUP, PW, J, ROWS, 128), f32),
        D((CH, J)), D((GROUP,)), D((GROUP,)), D((GROUP,)), D((GROUP,)), D((4,)), D((4,)),
        D((4,)), D((4,)), D((4,)), D((4,)), D((GROUP,)), D((GROUP,)), D((1,)),
    ]
    q1, cf, lo, hi, zl, zr, zo, gpk, arrived = pl.pallas_call(
        first_kernel,
        out_shape=(
            S(NT, J, 64, 128), S(J, 8, 9, 8, 128), S(CH, *edge), S(CH, *edge), S(CH, *packs), S(CH, *packs),
            S(CH, *packs), S(8, 128), S(GROUP, PW, J, ROWS, 128),
        ),
        in_specs=[smem, smem, vmem, vmem, vmem, hbm],
        out_specs=(hbm, vmem, hbm, hbm, hbm, hbm, vmem, vmem, hbm),
        scratch_shapes=scratch,
        compiler_params=pltpu.CompilerParams(
            collective_id=0, has_side_effects=True, vmem_limit_bytes=60 * 2**20
        ),
        name="first_substep",
    )(tile_dycore_slot, water_idx, dycore_air_mass, dycore_face_flux, weights, tracers)
    return pl.pallas_call(
        second_kernel,
        out_shape=(S(NT, 64, J * 128), S(SLOTS, NW, ROWS, J * 128)),
        in_specs=[smem, smem] + [vmem] * 9 + [hbm],
        out_specs=(hbm, vmem),
        scratch_shapes=[V((2, T, J, 80, 128), f32), V((2, T, J, 64, 128), f32), D((2,)), D((2, J))],
        compiler_params=pltpu.CompilerParams(vmem_limit_bytes=60 * 2**20),
        name="second_substep",
    )(tile_dycore_slot, water_idx, weights, cf, lo, hi, zl, zr, zo, gpk, arrived, q1)


def solution(mesh):
    return jax.shard_map(
        per_device,
        mesh=mesh,
        in_specs=(
            P("grp", "gx", "gy"),
            P(("grp", "gx", "gy"), None, None),
            P(("grp", "gx", "gy"), None, None, None),
            P(),
            P(),
        ),
        out_specs=(P("grp", "gx", "gy"), P(("grp", "gx", "gy"), None, None, None)),
        check_vma=False,
    )
```

time: 420 us -> 65.6 us (0.16); the launches traced: 415 us -> 65.1 us
  other arithmetic: 288 us -> 0 us
  Pallas kernels: 0 us -> 64.4 us
  waiting for transfers between devices: 51 us -> 0 us
  local copies, waits for them, and re-layouts: 40.8 us -> 0 us
  starting transfers between devices: 29.7 us -> 0 us
    mul x4 -> x0, other arithmetic: 133 us -> none  [upwind_faces(): return flow * jnp.where(flow > 0, from_left, from_right)]
    concatenate x3 -> x0, other arithmetic: 81.2 us -> none  [extended(): block = jnp.concatenate([low, block, high], axis=dim)]
    pallas_call x0 -> x2, Pallas kernels: none -> 64.4 us  [the longest x1 42.1 us: per_device(): pl.pallas_call(first_kernel, out_shape=(S(NT, J, 64, 128), S(J, 8, 9, 8,...]
    div x3 -> x0, other arithmetic: 55.6 us -> none  [the longest x2 55.6 us: advance(): (air_mass * centre - (flux_x[:, 1:] - flux_x[:, :-1]) - (flux_y[:, :, 1:]...]
    all_to_all x2 -> x0, waiting for transfers between devices: 27.4 us -> none  [per_device(): lax.all_to_all(outgoing, ('grp', 'gy'), split_axis=0, concat_axis=0, tile...]
    ppermute x8 -> x0, waiting for transfers between devices: 23.6 us -> none  [the longest x4 13.3 us: extended(): lax.ppermute(lax.slice_in_dim(block, 0, width, axis=dim), axis, backward)]
    ppermute x8 -> x0, starting transfers between devices: 19.6 us -> none  [the longest x4 9.82 us: extended(): lax.ppermute(lax.slice_in_dim(block, 0, width, axis=dim), axis, backward)]
    slice x3 -> x0, other arithmetic: 16.2 us -> none  [extended(): lax.slice_in_dim(block, block.shape[dim] - width, None, axis=dim)]
  transfers between devices with their start and end apart: 10 -> 0, of which waited for: 6 -> 0; matrix products, arithmetic and copies ran while one was open for 15% -> 0% of each run, Pallas kernels for 0% -> 0%
where the time goes in v1:
time: 65.6 us; the launch traced here: 65.1 us
  Pallas kernels  64.4 us (98%)
    pallas_call x1, Pallas kernels, per_device(): pl.pallas_call(first_kernel, out_shape=(S(NT, J, 64, 128), S(J, 8, 9, 8,...  42.1 us
    pallas_call x1, Pallas kernels, per_device(): pl.pallas_call(second_kernel, out_shape=(S(NT, 64, J * 128), S(SLOTS, NW,...  22.3 us

profile of v1, /device:TPU:96, one launch (start us, length us, event | category | flops | bytes accessed | tf_op | source)
XLA Modules:
  0.0 65.1 jit_solution(6403176095687335537)
XLA Ops:
  0.6 42.1 %first_substep.1 = (f32[128,3,64,128]{3,2,1,0:T(8,128)}, f32[3,8,9,8,128]{4,3,2,1,0:T(8,128)}, f32[16,48,128]{2,1,0:T(8,128)}, f32[16,48,128]{2,1,0:T(8,128)}, f...) custom-call(s32[256]{0:T(256)} %slot_ref.3, ...), custom_call_target="tpu_custom_call" | custom-call | tf_op jit(solution)/shard_map/first_substep/pallas_call | solution.py:578
  42.8 22.3 %second_substep.1 = (f32[128,64,384]{2,1,0:T(8,128)}, f32[4,6,16,384]{3,2,1,0:T(8,128)}) custom-call(s32[256]{0:T(256)} %slot_ref.3, s32[6]{0:T(128)} %water_ref.3, bf16[256,256]{1,0:T(8,128)(2,1)} %constant.2.clone.w_ref, f32[3,8,9,8,128]{4,3,2,1,0:T(8,128)} %get-tuple-element.11.cf, f32[16,48,128]{2,1,0:T(8,128)} %get-tuple-element.12.lo, ...), custom_call_target="tpu_custom_call" | custom-call | tf_op jit(solution)/shard_map/second_substep/pallas_call | solution.py:592

commit v2 on v1

--- a/solution.py
+++ b/solution.py
@@ -22,14 +22,17 @@
 NW = 6
 PW = 5
 EDGE = T * J * 2
+SET = T // 2 * J
 
 
 def stencil_weights():
-    w = np.zeros((256, 256), np.float32)
-    for b, taps in enumerate(({-1: -1, 0: 5, 1: 2}, {0: 2, 1: 5, 2: -1})):
+    w = np.zeros((256, 512), np.float32)
+    for b, (shift, taps) in enumerate(
+        (s, t) for s in (0, -1) for t in ({-1: -1, 0: 5, 1: 2}, {0: 2, 1: 5, 2: -1})
+    ):
         for n in range(128):
             for d, v in taps.items():
-                y = n + d
+                y = n + d + shift
                 if 0 <= y < 128:
                     w[y, b * 128 + n] += v
                     if 2 <= y < 126:
@@ -62,59 +65,66 @@
     return jnp.where((lanes() & 3) < 2, left, right)
 
 
-def left_faces(left, own, flow):
-    y = merge_edges(left, own)
-    y1, y2, y3 = pltpu.roll(y, 1, 1), pltpu.roll(y, 2, 1), pltpu.roll(y, 3, 1)
-    return flow * jnp.where(flow > 0, 5.0 * y2 + (2.0 * y1 - y3), 2.0 * y2 + (5.0 * y1 - y))
-
-
-def advance(q, cf, sub, w, edges, faces, put, count, packed):
+def load_weights(w_ref, accs):
+    for m in range(2):
+        pltpu.matmul_push_rhs(w_ref[:, 256 * m : 256 * m + 256], 0, m)
+        pltpu.matmul_acc_lhs(accs[m][0], jnp.zeros((16, 256), bf16), load_staged_rhs=0)
+        pltpu.matmul_pop(accs[m][0])
+
+
+def issue_row(q, accs, base, edges, count, xg):
     lane16 = lax.broadcasted_iota(jnp.int32, (16, 128), 1)
-    lane = lanes()
     half16 = lane16 < 64
     edge16 = (lane16 < 2) | (lane16 >= 126)
-    main, second = [], []
+    for t in range(0, count, 2):
+        ts = [t, min(t + 1, count - 1)]
+        both = [cat(*[q(u, j, 8 * xg) for u in ts]) for j in range(J)]
+        outer = cat(*[pltpu.roll(edges[u // 4], (254 - place(u, xg)) % 128, 1) for u in ts]).astype(bf16)
+        high = [a.astype(bf16) for a in both]
+        for j in range(J):
+            left = outer if j == 0 else high[j - 1]
+            right = outer if j == J - 1 else high[j + 1]
+            low = (both[j] - high[j].astype(f32)).astype(bf16)
+            second = jnp.where(edge16, jnp.where(half16, right, left), low)
+            lhs = jnp.concatenate([high[j], second], 1)
+            for m in range(2):
+                pltpu.matmul_acc_lhs(accs[m][base], lhs)
+            base += 1
+
+
+def finish_row(q, cf, sub, accs, base, put, count, xg, packed):
+    for t in range(0, count, 2):
+        new = {}
+        for j in range(J):
+            c = [cf[j, xg, 7 * sub + k] for k in range(7)]
+            upper, lower = (pltpu.matmul_pop(accs[m][base]) for m in range(2))
+            base += 1
+            for u in range(min(2, count - t)):
+                r = slice(8 * u, 8 * u + 8)
+                x = [q(t + u, j, 8 * xg + d) for d in (-2, -1, 0, 1, 2)]
+                s = (c[0] * x[0] + c[1] * x[1]) + (c[2] * x[2] + c[3] * x[3])
+                v = c[4] * x[4] + c[5] * jnp.where(c[5] < 0, upper[r, :128], upper[r, 128:])
+                v = v + c[6] * jnp.where(c[6] > 0, lower[r, :128], lower[r, 128:])
+                new[u, j] = s + v
+                put(t + u, j, xg, new[u, j])
+        if packed is not None:
+            for u in range(min(2, count - t)):
+                k = (t + u) // 4
+                packed[k] = pack_edges(packed[k], t + u, xg, new[u, 0], new[u, J - 1])
+
+
+def advance(q, cf, sub, accs, edges, put, count, packed):
+    issue_row(q, accs, 0, edges, count, 0)
     for xg in range(8):
-        for t in range(0, count, 2):
-            ts = [t, min(t + 1, count - 1)]
-            av = [cat(*[q(u, j, 8 * xg) for u in ts]) for j in range(J)]
-            uv = cat(*[pltpu.roll(edges[u // 4], (254 - place(u, xg)) % 128, 1) for u in ts]).astype(bf16)
-            high = [a.astype(bf16) for a in av]
-            for j in range(J):
-                left = uv if j == 0 else high[j - 1]
-                right = uv if j == J - 1 else high[j + 1]
-                low = (av[j] - high[j].astype(f32)).astype(bf16)
-                main.append(high[j])
-                second.append(jnp.where(edge16, jnp.where(half16, right, left), low))
-    lhs = jnp.concatenate([jnp.concatenate(main, 0), jnp.concatenate(second, 0)], 1)
-    both = jnp.dot(lhs, w, preferred_element_type=f32)
-    row = 0
-    for xg in range(8):
-        for t in range(0, count, 2):
-            for u in range(2):
-                if t + u >= count:
-                    continue
-                flux, moved = [], []
-                for j in range(J):
-                    r = slice((row + j) * 16 + u * 8, (row + j) * 16 + u * 8 + 8)
-                    f = cf[j, xg, 4]
-                    flux.append(f * jnp.where(f > 0, both[r, :128], both[r, 128:]))
-                    moved.append(pltpu.roll(flux[j], 1, 1))
-                before = pltpu.roll(faces[(t + u) // 4], (253 - place(t + u, xg)) % 128, 1)
-                new = []
-                for j in range(J):
-                    x = [q(t + u, j, 8 * xg + d) for d in (-2, -1, 0, 1, 2)]
-                    c = [cf[j, xg, k] for k in range(4)]
-                    s = (c[0] * x[0] + c[1] * x[1]) + (c[2] * x[3] + c[3] * x[4])
-                    v = cf[j, xg, 5 + 2 * sub] * x[2] - flux[j]
-                    v = v + jnp.where(lane == 0, before if j == 0 else moved[j - 1], moved[j])
-                    new.append((s + v) * cf[j, xg, 6 + 2 * sub])
-                    put(t + u, j, xg, new[j])
-                if packed is not None:
-                    k = (t + u) // 4
-                    packed[k] = pack_edges(packed[k], t + u, xg, new[0], new[J - 1])
-            row += J
+        if xg < 7:
+            issue_row(q, accs, (xg + 1) % 2 * SET, edges, count, xg + 1)
+        finish_row(q, cf, sub, accs, xg % 2 * SET, put, count, xg, packed)
     return packed
+
+
+def with_accumulators(body):
+    n = 2 * SET
+    pl.run_scoped(lambda *a: body((a[:n], a[n:])), *[pltpu.ACC(i // n)((16, 256), f32) for i in range(2 * n)])
 
 
 def total(items):
@@ -136,10 +146,15 @@
     return ids, halves, ranks
 
 
-def first_kernel(
+def first_kernel(*refs):
+    with_accumulators(lambda accs: first_body(accs, *refs))
+
+
+def first_body(
+    accs,
     slot_ref, water_ref, mass_ref, flux_ref, w_ref, tracers,
-    q1, cf, lo2, hi2, zl2, zr2, z1, gpk, arrived,
-    q0, q1v, up1, dn1, lo1, hi1, z0, zl1, zr1, up2, dn2, tsend, trecv, xsend, xrecv,
+    q1, cf, lo2, hi2, zl2, zr2, arrived,
+    q0, q1v, z1, up1, dn1, lo1, hi1, z0, zl1, zr1, up2, dn2, tsend, trecv, xsend, xrecv,
     mass, fx, fy, qw, qw1, upw, dnw, low, hiw, zw, zlw, zrw, q2w, wsend,
     load_sem, tile_ssem, tile_rsem, row_ssem, row_rsem, halo_ssem, halo_rsem,
     next_ssem, next_rsem, wh_ssem, wh_rsem, ws_sem, wr_sem, out_sem,
@@ -168,6 +183,7 @@
         return 0
 
     lax.fori_loop(0, CH, start_load, 0)
+    load_weights(w_ref, accs)
 
     barrier = pltpu.get_barrier_semaphore()
 
@@ -331,10 +347,6 @@
     for j in range(J):
         v = jnp.where(gx > 0, xrecv[k, pl.ds(j, 1), :] * (1.0 / 12.0), 0.0)
         fx[j, pl.ds(7, 1), :] = v
-    g = jnp.zeros((8, 128), f32)
-    for xg in range(8):
-        g = jnp.where(lane == 4 * xg + 3, pltpu.roll(left[xg], 4 * xg + 4, 1), g)
-    gpk[...] = (g + pltpu.roll(g, 32, 1)) + (pltpu.roll(g, 64, 1) + pltpu.roll(g, 96, 1))
     for xg in range(8):
         moved = []
         for j in range(J):
@@ -344,20 +356,18 @@
             h = fy[j, pl.ds(8 * xg, 8), :]
             moved.append(pltpu.roll(h, 1, 1))
             last = pltpu.roll(left[xg], 1, 1) if j == 0 else moved[j - 1]
-            out = 6.0 * ((f - b) + (h - jnp.where(lane == 0, last, moved[j])))
+            h0 = jnp.where(lane == 0, last, moved[j])
+            out = 6.0 * ((f - b) + (h - h0))
             m0 = mass[j, pl.ds(8 * xg, 8), :]
-            m1 = m0 - out
-            m2 = m1 - out
             centre = (5.0 * fp + 2.0 * fm) - (2.0 * gp + 5.0 * gm)
-            cf[j, xg, 0] = -gp
-            cf[j, xg, 1] = fp + (5.0 * gp + 2.0 * gm)
-            cf[j, xg, 2] = -(2.0 * fp + 5.0 * fm) - gm
-            cf[j, xg, 3] = fm
-            cf[j, xg, 4] = h
-            cf[j, xg, 5] = m0 - centre
-            cf[j, xg, 6] = 1.0 / m1
-            cf[j, xg, 7] = m1 - centre
-            cf[j, xg, 8] = 1.0 / m2
+            for sub in range(2):
+                m1 = m0 - out
+                inv = 1.0 / m1
+                for k, v in enumerate(
+                    (-gp, fp + (5.0 * gp + 2.0 * gm), m0 - centre, -(2.0 * fp + 5.0 * fm) - gm, fm, -h, h0)
+                ):
+                    cf[j, xg, 7 * sub + k] = v * inv
+                m0 = m1
 
     wait_sets(sets1, halo_ssem, halo_rsem, True)
 
@@ -366,22 +376,22 @@
             dst(t, j, 6, jnp.where(get[0], lo[c, pl.ds(r, 2), :], 0.0))
             dst(t, j, 72, jnp.where(get[1], hi[c, pl.ds(r, 2), :], 0.0))
 
-    def edge_terms(zl, zr, zo, c):
-        zls = [jnp.where(get[2], zl[c, k], 0.0) for k in range(2)]
-        zrs = [jnp.where(get[3], zr[c, k], 0.0) for k in range(2)]
-        return [merge_edges(a, b) for a, b in zip(zls, zrs)], [left_faces(zls[k], zo[c, k], gpk[...]) for k in range(2)]
+    def edge_terms(zl, zr, c):
+        return [
+            merge_edges(jnp.where(get[2], zl[c, k], 0.0), jnp.where(get[3], zr[c, k], 0.0)) for k in range(2)
+        ]
 
     def put_qw(t, j, r, v):
         qw[t, j, pl.ds(r, 2), :] = v
 
     fill(put_qw, CH, PW, lo1, hi1)
-    edges, faces = edge_terms(zl1, zr1, z0, CH)
+    edges = edge_terms(zl1, zr1, CH)
 
     def put_qw1(t, j, xg, v):
         qw1[t, j, pl.ds(8 + 8 * xg, 8), :] = v
 
     packed = advance(
-        lambda t, j, r: qw[t, j, pl.ds(8 + r, 8), :], cf, 0, w_ref[...], edges, faces, put_qw1, PW,
+        lambda t, j, r: qw[t, j, pl.ds(8 + r, 8), :], cf, 0, accs, edges, put_qw1, PW,
         [jnp.zeros((8, 128), f32)] * 2,
     )
     for k in range(2):
@@ -411,13 +421,13 @@
             qw1[t, j, pl.ds(r, 2), :] = v
 
         fill(put_halo, 0, PW, low, hiw)
-        edges, faces = edge_terms(zlw, zrw, zw, 0)
+        edges = edge_terms(zlw, zrw, 0)
 
         def put_q2(t, j, xg, v):
             q2w[xg // 2, t, j, pl.ds(8 * (xg % 2), 8), :] = v
 
         advance(
-            lambda t, j, r: qw1[t, j, pl.ds(8 + r, 8), :], cf, 1, w_ref[...], edges, faces, put_q2, PW, None
+            lambda t, j, r: qw1[t, j, pl.ds(8 + r, 8), :], cf, 1, accs, edges, put_q2, PW, None
         )
         for k in range(GROUP):
             p = peer(k)
@@ -438,13 +448,13 @@
             q0[c * T + t, j, pl.ds(r, 2), :] = v
 
         fill(put_q0, c, T, lo1, hi1)
-        edges, faces = edge_terms(zl1, zr1, z0, c)
+        edges = edge_terms(zl1, zr1, c)
 
         def put_q1(t, j, xg, v):
             q1v[c * T + t, j, pl.ds(8 * xg, 8), :] = v
 
         packed = advance(
-            lambda t, j, r: q0[c * T + t, j, pl.ds(8 + r, 8), :], cf, 0, w_ref[...], edges, faces, put_q1, T,
+            lambda t, j, r: q0[c * T + t, j, pl.ds(8 + r, 8), :], cf, 0, accs, edges, put_q1, T,
             [jnp.zeros((8, 128), f32)] * 2,
         )
         for k in range(2):
@@ -481,23 +491,34 @@
         water_copy(k).wait()
 
 
-def second_kernel(
-    slot_ref, water_ref, w_ref, cf, lo, hi, zl, zr, zo, gpk, arrived, q1,
+def second_kernel(*refs):
+    with_accumulators(lambda accs: second_body(accs, *refs))
+
+
+def second_body(
+    accs,
+    slot_ref, water_ref, w_ref, cf, lo, hi, zl, zr, arrived, q1,
     out, water, qb, ob, in_sem, out_sem,
 ):
     grp, gx, gy = lax.axis_index("grp"), lax.axis_index("gx"), lax.axis_index("gy")
     me = (grp * NX + gx) * NY + gy
     pos = grp * NY + gy
 
-    def load(c, s):
-        return pltpu.make_async_copy(q1.at[pl.ds(c * T, T)], qb.at[s, :, :, pl.ds(8, 64), :], in_sem.at[s])
-
-    def store(c, s, j):
-        return pltpu.make_async_copy(
-            ob.at[s, :, j], out.at[pl.ds(c * T, T), :, pl.ds(128 * j, 128)], out_sem.at[s, j]
-        )
-
-    load(0, 0).start()
+    def load(c):
+        return pltpu.make_async_copy(q1.at[pl.ds(c * T, T)], qb.at[pl.ds(c * T, T), :, pl.ds(8, 64), :], in_sem.at[c])
+
+    def store(c):
+        return pltpu.make_async_copy(ob.at[pl.ds(c * T, T)], out.at[pl.ds(c * T, T)], out_sem.at[c])
+
+    def each(body):
+        def step(c, _):
+            body(c)
+            return 0
+
+        lax.fori_loop(0, CH, step, 0)
+
+    each(lambda c: load(c).start())
+    load_weights(w_ref, accs)
 
     ids, halves, ranks = water_places(water_ref)
     for s in range(SLOTS):
@@ -512,42 +533,25 @@
             for j in range(J):
                 water[s, w, :, 128 * j : 128 * j + 128] = jnp.where(valid > 0, arrived[k, ranks[w], j], 0.0)
 
-    def chunk(c, _):
-        s = lax.rem(c, 2)
-
-        @pl.when(c + 1 < CH)
-        def _():
-            load(c + 1, 1 - s).start()
-
-        load(c, s).wait()
-
-        @pl.when(c >= 2)
-        def _():
-            for j in range(J):
-                store(c - 2, s, j).wait()
-
+    def chunk(c):
+        load(c).wait()
         for t in range(T):
             for j in range(J):
                 r = (t * J + j) * 2
-                qb[s, t, j, pl.ds(6, 2), :] = jnp.where(gx > 0, lo[c, pl.ds(r, 2), :], 0.0)
-                qb[s, t, j, pl.ds(72, 2), :] = jnp.where(gx < NX - 1, hi[c, pl.ds(r, 2), :], 0.0)
-        zls = [jnp.where(gy > 0, zl[c, k], 0.0) for k in range(2)]
-        zrs = [jnp.where(gy < NY - 1, zr[c, k], 0.0) for k in range(2)]
-        edges = [merge_edges(a, b) for a, b in zip(zls, zrs)]
-        faces = [left_faces(zls[k], zo[c, k], gpk[...]) for k in range(2)]
+                qb[c * T + t, j, pl.ds(6, 2), :] = jnp.where(gx > 0, lo[c, pl.ds(r, 2), :], 0.0)
+                qb[c * T + t, j, pl.ds(72, 2), :] = jnp.where(gx < NX - 1, hi[c, pl.ds(r, 2), :], 0.0)
+        edges = [
+            merge_edges(jnp.where(gy > 0, zl[c, k], 0.0), jnp.where(gy < NY - 1, zr[c, k], 0.0)) for k in range(2)
+        ]
 
         def put(t, j, xg, v):
-            ob[s, t, j, pl.ds(8 * xg, 8), :] = v
-
-        advance(lambda t, j, r: qb[s, t, j, pl.ds(8 + r, 8), :], cf, 1, w_ref[...], edges, faces, put, T, None)
-        for j in range(J):
-            store(c, s, j).start()
-        return 0
-
-    lax.fori_loop(0, CH, chunk, 0)
-    for c in (CH - 2, CH - 1):
-        for j in range(J):
-            store(c, c % 2, j).wait()
+            ob[c * T + t, pl.ds(8 * xg, 8), 128 * j : 128 * j + 128] = v
+
+        advance(lambda t, j, r: qb[c * T + t, j, pl.ds(8 + r, 8), :], cf, 1, accs, edges, put, T, None)
+        store(c).start()
+
+    each(chunk)
+    each(lambda c: store(c).wait())
 
 
 def per_device(tracers, dycore_air_mass, dycore_face_flux, tile_dycore_slot, water_idx):
@@ -562,7 +566,7 @@
 
     edge, packs = (EDGE, 128), (2, 8, 128)
     scratch = [
-        V((NT, J, 80, 128), f32), V((NT, J, 64, 128), f32),
+        V((NT, J, 80, 128), f32), V((NT, J, 64, 128), f32), V((CH, *packs), f32),
         V((CH + 1, *edge), f32), V((CH + 1, *edge), f32), V((CH + 1, *edge), f32), V((CH + 1, *edge), f32),
         V((CH + 1, *packs), f32), V((CH + 1, *packs), f32), V((CH + 1, *packs), f32),
         V((CH, *edge), f32), V((CH, *edge), f32),
@@ -575,14 +579,14 @@
         D((CH, J)), D((GROUP,)), D((GROUP,)), D((GROUP,)), D((GROUP,)), D((4,)), D((4,)),
         D((4,)), D((4,)), D((4,)), D((4,)), D((GROUP,)), D((GROUP,)), D((1,)),
     ]
-    q1, cf, lo, hi, zl, zr, zo, gpk, arrived = pl.pallas_call(
+    q1, cf, lo, hi, zl, zr, arrived = pl.pallas_call(
         first_kernel,
         out_shape=(
-            S(NT, J, 64, 128), S(J, 8, 9, 8, 128), S(CH, *edge), S(CH, *edge), S(CH, *packs), S(CH, *packs),
-            S(CH, *packs), S(8, 128), S(GROUP, PW, J, ROWS, 128),
+            S(NT, J, 64, 128), S(J, 8, 14, 8, 128), S(CH, *edge), S(CH, *edge), S(CH, *packs), S(CH, *packs),
+            S(GROUP, PW, J, ROWS, 128),
         ),
         in_specs=[smem, smem, vmem, vmem, vmem, hbm],
-        out_specs=(hbm, vmem, hbm, hbm, hbm, hbm, vmem, vmem, hbm),
+        out_specs=(hbm, vmem, hbm, hbm, hbm, hbm, hbm),
         scratch_shapes=scratch,
         compiler_params=pltpu.CompilerParams(
             collective_id=0, has_side_effects=True, vmem_limit_bytes=60 * 2**20
@@ -592,12 +596,12 @@
     return pl.pallas_call(
         second_kernel,
         out_shape=(S(NT, 64, J * 128), S(SLOTS, NW, ROWS, J * 128)),
-        in_specs=[smem, smem] + [vmem] * 9 + [hbm],
+        in_specs=[smem, smem] + [vmem] * 7 + [hbm],
         out_specs=(hbm, vmem),
-        scratch_shapes=[V((2, T, J, 80, 128), f32), V((2, T, J, 64, 128), f32), D((2,)), D((2, J))],
+        scratch_shapes=[V((NT, J, 80, 128), f32), V((NT, 64, J * 128), f32), D((CH,)), D((CH,))],
         compiler_params=pltpu.CompilerParams(vmem_limit_bytes=60 * 2**20),
         name="second_substep",
-    )(tile_dycore_slot, water_idx, weights, cf, lo, hi, zl, zr, zo, gpk, arrived, q1)
+    )(tile_dycore_slot, water_idx, weights, cf, lo, hi, zl, zr, arrived, q1)
 
 
 def solution(mesh):

time: 65.6 us -> 60.8 us (0.927)
  Pallas kernels: 64.4 us -> 60 us
    pallas_call x1, Pallas kernels: 22.3 us -> 17.8 us  [per_device(): pl.pallas_call(second_kernel, out_shape=(S(NT, 64, J * 128), S(SLOTS, NW,...]
where the time goes in v2:
time: 60.8 us; the launch traced here: 60.6 us
  Pallas kernels  60 us (99%)
  between operations  0.64 us (1%)
    pallas_call x1, Pallas kernels, per_device(): pl.pallas_call(first_kernel, out_shape=(S(NT, J, 64, 128), S(J, 8, 14, 8,...  42.1 us
    pallas_call x1, Pallas kernels, per_device(): pl.pallas_call(second_kernel, out_shape=(S(NT, 64, J * 128), S(SLOTS, NW,...  17.8 us

profile of v2, /device:TPU:96, one launch (start us, length us, event | category | flops | bytes accessed | tf_op | source)
XLA Modules:
  0.0 60.6 jit_solution(6596599517753050014)
XLA Ops:
  0.6 42.1 %first_substep.1 = (f32[128,3,64,128]{3,2,1,0:T(8,128)}, f32[3,8,14,8,128]{4,3,2,1,0:T(8,128)}, f32[16,48,128]{2,1,0:T(8,128)}, f32[16,48,128]{2,1,0:T(8,128)}, ...) custom-call(s32[256]{0:T(256)} %refs_0_.3, s32[6]{0:T(128)} %refs_1_.3, ...), custom_call_target="tpu_custom_call" | custom-call | tf_op jit(solution)/shard_map/first_substep/pallas_call | solution.py:582
  42.8 17.8 %second_substep.1 = (f32[128,64,384]{2,1,0:T(8,128)}, f32[4,6,16,384]{3,2,1,0:T(8,128)}) custom-call(s32[256]{0:T(256)} %refs_0_.3, s32[6]{0:T(128)} %refs_1_.3, bf16[256,512]{1,0:T(8,128)(2,1)} %constant.2.clone.refs_4_.refs_2_, f32[3,8,14,8,128]{4,3,2,1,0:T(8,128)} %get-tuple-element.9.refs_3_, f32[16,48,128]{2,1,0:T(8,128)} %get-tuple-element.10.refs_4_, ...), custom_call_target="tpu_custom_call" | custom-call | tf_op jit(solution)/shard_map/second_substep/pallas_call | solution.py:596
